TPU v7x, 256 devices: a whole 4x4x8 slice. The times are simulated.
256 devices in a mesh: ctx: 8 (over z), head: 4 (over y_hi, core), sess: 8 (over y_lo, x).
Axes of the slice: x: 4, y: 4 (y_hi: 2, y_lo: 2; y = y_hi * 2 + y_lo), z: 8, core: 2. Of those that a mesh axis runs over, the one named last changes fastest.
Arguments:
- queries: bfloat16 [512, 64, 128], P(('ctx', 'sess'), 'head'), may hold values from -300 to 300
- prefix_keys: bfloat16 [8, 49152, 128], P('head', 'ctx'), may hold values from -5 to 5
- prefix_values: bfloat16 [8, 49152, 128], P('head', 'ctx'), may hold values from -6 to 6
- suffix_keys: bfloat16 [512, 8, 512, 128], P(('ctx', 'sess'), 'head'), may hold values from -7 to 7
- suffix_values: bfloat16 [512, 8, 512, 128], P(('ctx', 'sess'), 'head'), may hold values from -6 to 6
- lengths: int32 [512], P(('ctx', 'sess')), may hold values from 1 to 512, as said below
- out_weight: bfloat16 [8192, 8192], P('head', ('ctx', 'sess')), may hold values from -0.0625 to 0.0625
Outputs:
- layer_out: float32 [512, 8192], P('head', ('ctx', 'sess'))
Inputs may be any that keep to these rules, and one draw needn't show every extreme that they name: `lengths`: every session has at least one live suffix token; some session has exactly 512.
All inputs are finite; a program needn't handle non-finite values.
Results may differ from a plain program's by a relative error of at most 0.0065.
Values may be sent and summed in bfloat16 or wider, within the bound.
No kernel may reach another device: no remote copies, remote signals or barrier semaphores. Data moves between devices by JAX's collectives and lax.ppermute only.
A program may use at most 64 MiB of HBM per device.

v0:
```python
import math
import jax
import jax.numpy as jnp
from jax import lax
from jax.sharding import PartitionSpec as P


def online_update(state_carry, scores, values, einsum_form):
    run_max, run_sum, numerator = state_carry
    new_max = jnp.maximum(run_max, jnp.max(scores, axis=-1))
    factor = jnp.exp(run_max - new_max)
    weights = jnp.exp(scores - new_max[..., None])
    new_sum = run_sum * factor + jnp.sum(weights, axis=-1)
    product = jnp.einsum(
        einsum_form, weights.astype(jnp.bfloat16), values, preferred_element_type=jnp.float32
    )
    return (new_max, new_sum, numerator * factor[..., None] + product)


def per_device(
    queries, prefix_keys, prefix_values, suffix_keys, suffix_values, lengths, out_weight
):
    own_rows = queries.shape[0]
    kv_local = prefix_keys.shape[0]
    head_dim = queries.shape[2]
    group_size = queries.shape[1] // kv_local
    score_scale = 1.0 / math.sqrt(head_dim)
    gathered = lax.all_gather(queries, "ctx", axis=0, tiled=True)
    rows_total = gathered.shape[0]
    grouped = gathered.reshape(rows_total, kv_local, group_size, head_dim)
    prefix_len = prefix_keys.shape[1]
    key_block_len = min(512, prefix_len)

    def prefix_step(state_carry, block_index):
        first_key = block_index * key_block_len
        key_block = lax.dynamic_slice_in_dim(prefix_keys, first_key, key_block_len, 1)
        value_block = lax.dynamic_slice_in_dim(prefix_values, first_key, key_block_len, 1)
        scores = (
            jnp.einsum("rkgd,knd->rkgn", grouped, key_block, preferred_element_type=jnp.float32)
            * score_scale
        )
        return (online_update(state_carry, scores, value_block, "rkgn,knd->rkgd"), None)

    start_state = (
        jnp.full((rows_total, kv_local, group_size), -1e30, jnp.float32),
        jnp.zeros((rows_total, kv_local, group_size), jnp.float32),
        jnp.zeros((rows_total, kv_local, group_size, head_dim), jnp.float32),
    )
    prefix_state, unused = lax.scan(
        prefix_step, start_state, jnp.arange(prefix_len // key_block_len, dtype=jnp.int32)
    )
    run_max, run_sum, numerator = prefix_state
    max_parts, sum_parts, numer_parts = (
        lax.all_to_all(run_max, "ctx", split_axis=0, concat_axis=0, tiled=True),
        lax.all_to_all(run_sum, "ctx", split_axis=0, concat_axis=0, tiled=True),
        lax.all_to_all(numerator, "ctx", split_axis=0, concat_axis=0, tiled=True),
    )
    sources = max_parts.shape[0] // own_rows
    max_parts = max_parts.reshape(sources, own_rows, kv_local, group_size)
    sum_parts = sum_parts.reshape(sources, own_rows, kv_local, group_size)
    numer_parts = numer_parts.reshape(sources, own_rows, kv_local, group_size, head_dim)
    row_top = jnp.max(max_parts, axis=0)
    rescale = jnp.exp(max_parts - row_top[None])
    merged_sum = jnp.sum(sum_parts * rescale, axis=0)
    merged_numer = jnp.sum(numer_parts * rescale[..., None], axis=0)
    own_queries = queries.reshape(own_rows, kv_local, group_size, head_dim)
    suffix_len = suffix_keys.shape[2]
    suffix_block = min(128, suffix_len)
    block_total = (jnp.max(lengths) + suffix_block - 1) // suffix_block

    def suffix_step(block_index, state_carry):
        first_key = block_index * suffix_block
        key_block = lax.dynamic_slice_in_dim(suffix_keys, first_key, suffix_block, 2)
        value_block = lax.dynamic_slice_in_dim(suffix_values, first_key, suffix_block, 2)
        scores = (
            jnp.einsum(
                "skgd,sknd->skgn", own_queries, key_block, preferred_element_type=jnp.float32
            )
            * score_scale
        )
        position = first_key + jnp.arange(suffix_block, dtype=jnp.int32)
        live_mask = position[None, :] < lengths[:, None]
        scores = jnp.where(live_mask[:, None, None, :], scores, -1e30)
        return online_update(state_carry, scores, value_block, "skgn,sknd->skgd")

    final_state = lax.fori_loop(0, block_total, suffix_step, (row_top, merged_sum, merged_numer))
    attended = (final_state[2] / final_state[1][..., None]).astype(jnp.bfloat16)
    attended = attended.reshape(own_rows, kv_local * group_size * head_dim)
    partial_out = jnp.dot(
        lax.all_gather(attended, ("ctx", "sess"), axis=0, tiled=True),
        out_weight,
        preferred_element_type=jnp.float32,
    )
    return lax.psum_scatter(partial_out, "head", scatter_dimension=0, tiled=True)


def solution(mesh):
    return jax.shard_map(
        per_device,
        mesh=mesh,
        in_specs=(
            P(("ctx", "sess"), "head", None),
            P("head", "ctx", None),
            P("head", "ctx", None),
            P(("ctx", "sess"), "head", None, None),
            P(("ctx", "sess"), "head", None, None),
            P(("ctx", "sess")),
            P("head", ("ctx", "sess")),
        ),
        out_specs=P("head", ("ctx", "sess")),
        check_vma=False,
    )
```

profile of v0, /device:TPU:1, one launch (start us, length us, event | category | flops | bytes accessed | tf_op | source)
XLA Modules:
  0.0 490.1 jit_solution(15948177267286865824)
XLA Ops:
  6.5 23.6 %all_gather.6 = bf16[64,16,128]{2,1,0:T(8,128)(2,1)S(1)} all-gather(bf16[8,16,128]{2,1,0:T(8,128)(2,1)} %param.11), channel_id=1, replica_groups=mesh['ctx'=8,'head'=4,'sess'=8] {'ctx'}, dimensions={0}, use_global_device_ids=true | all-gather | bytes 294912 | tf_op jit(solution)/shard_map/all_gather | solution.py:28
  30.2 63.2 %while.30 = (s32[]{:T(128)}, f32[64,2,8]{0,2,1:T(8,128)S(1)}, f32[64,2,8]{0,2,1:T(8,128)S(1)}, f32[64,2,8,128]{3,0,2,1:T(8,128)S(1)}, s32[12]{0:T(128)S(1)}, /*i...) while((s32[]{:T(128)}, f32[64,2,8]{0,2,1:T(8,128)S(1)}, ...), condition=%wide.region_3.4_spmd.clone, body=%wide.region_0.3_spmd.clone.sunk | while | flops 273028096 | bytes 8192195 | solution.py:49
  33.7 1.8 fusion.55
  39.0 1.8 fusion.55
  44.3 1.8 fusion.55
  49.5 1.8 fusion.55
  54.8 1.8 fusion.55
  60.1 1.8 fusion.55
  65.3 1.8 fusion.55
  70.6 1.8 fusion.55
  75.8 1.8 fusion.55
  81.1 1.8 fusion.55
  86.4 1.8 fusion.55
  91.6 1.8 fusion.55
  94.3 4.6 all-to-all-start
  99.7 5.6 %all-to-all-done = f32[8,1,128]{2,1,0:T(1,128)S(1)} async-done(((f32[8,1,128]{2,1,0:T(1,128)}), f32[8,1,128]{2,1,0:T(1,128)S(1)}, u32[]{:S(2)}, u32[]{:S(2)}) %all-to-all-start) | async-done | bytes 4128 | tf_op jit(solution)/shard_map/all_to_all | solution.py:54
  105.3 3.3 all-to-all-start.1
  109.8 5.3 %all-to-all-done.1 = f32[8,1,128]{2,1,0:T(1,128)S(1)} async-done(((f32[8,1,128]{2,1,0:T(1,128)}), f32[8,1,128]{2,1,0:T(1,128)S(1)}, u32[]{:S(2)}, u32[]{:S(2)}) %all-to-all-start.1) | async-done | bytes 4128 | tf_op jit(solution)/shard_map/all_to_all | solution.py:55
  115.1 3.5 all-to-all-start.2
  122.4 8.3 %all-to-all-done.2 = f32[64,2,8,128]{3,2,1,0:T(8,128)S(1)} async-done(((f32[64,2,8,128]{3,2,1,0:T(8,128)}), f32[64,2,8,128]{3,2,1,0:T(8,128)S(1)}, u32[]{:S(2)}, u32[]{:S(2)}) %all-to-all-start.2) | async-done | bytes 524320 | tf_op jit(solution)/shard_map/all_to_all | solution.py:56
  130.9 12.8 %while.29 = (s32[]{:T(128)}, f32[8,2,8]{2,1,0:T(2,128)S(1)}, f32[8,2,8]{2,1,0:T(2,128)S(1)}, f32[8,2,8,128]{3,2,1,0:T(8,128)S(1)}, s32[]{:T(128)}, /*index=5*/s3...) while((s32[]{:T(128)}, f32[8,2,8]{2,1,0:T(2,128)S(1)}, ...), condition=%wide.region_11.12_spmd, body=%wide.region_8.11_spmd.sunk | while | flops 8537478 | bytes 1420503 | solution.py:86
  144.5 261.2 %all-gather.2.cloned.1.call-done = bf16[512,2048]{1,0:T(8,128)(2,1)} async-done(((bf16[8,2048]{1,0:T(8,128)(2,1)}), bf16[512,2048]{1,0:T(8,128)(2,1)}) %all-gather.2.cloned.1.call-update) | async-done | bytes 2097168 | tf_op jit(solution)/shard_map/all_gather | solution.py:90
  405.7 3.0 fusion.29
  408.8 74.5 %reduce-scatter.2.cloned.1.call-done = f32[128,128]{1,0:T(8,128)} async-done(((f32[512,128]{1,0:T(8,128)}), f32[128,128]{1,0:T(8,128)}) %reduce-scatter.2.cloned.1.call-update) | async-done | bytes 65552 | tf_op jit(solution)/shard_map/reduce_scatter | solution.py:94
  (140 shorter events, 52.6 us)
Async XLA Ops:
  6.5 399.2 %copy-start = (bf16[2048,128]{1,0:T(8,128)(2,1)S(1)}, bf16[2048,128]{1,0:T(8,128)(2,1)}, u32[]{:S(2)}) copy-start(bf16[2048,128]{1,0:T(8,128)(2,1)} %param.17) | copy-start | bytes 1572868
  93.4 25.2 %copy-start.2 = (s32[8]{0:T(128)S(1)}, s32[8]{0:T(128)}, u32[]{:S(2)}) copy-start(s32[8]{0:T(128)} %param.16) | copy-start | bytes 100
  93.4 37.5 %copy-start.1 = (bf16[8,16,128]{2,1,0:T(8,128)(2,1)S(1)}, bf16[8,16,128]{2,1,0:T(8,128)(2,1)}, u32[]{:S(2)}) copy-start(bf16[8,16,128]{2,1,0:T(8,128)(2,1)} %param.11) | copy-start | bytes 98308
  94.3 11.0 %all-to-all-start = ((f32[8,1,128]{2,1,0:T(1,128)}), f32[8,1,128]{2,1,0:T(1,128)S(1)}, u32[]{:S(2)}, u32[]{:S(2)}) async-start(f32[8,1,128]{2,1,0:T(1,128)} %reshape.67), calls=%async_computation | async-start | bytes 8192 | tf_op jit(solution)/shard_map/all_to_all | solution.py:54
  105.3 9.8 %all-to-all-start.1 = ((f32[8,1,128]{2,1,0:T(1,128)}), f32[8,1,128]{2,1,0:T(1,128)S(1)}, u32[]{:S(2)}, u32[]{:S(2)}) async-start(f32[8,1,128]{2,1,0:T(1,128)} %reshape.69), calls=%async_computation.1 | async-start | bytes 8192 | tf_op jit(solution)/shard_map/all_to_all | solution.py:55
  115.1 15.6 %all-to-all-start.2 = ((f32[64,2,8,128]{3,2,1,0:T(8,128)}), f32[64,2,8,128]{3,2,1,0:T(8,128)S(1)}, u32[]{:S(2)}, u32[]{:S(2)}) async-start(f32[64,2,8,128]{3,2,1,0:T(8,128)} %copy.16), calls=%async_computation.2 | async-start | bytes 1048576 | tf_op jit(solution)/shard_map/all_to_all | solution.py:56
  118.6 287.1 %all-gather.2.cloned.1.call-start = ((), (), s32[]{:S(2)}) async-start(), calls=%async_computation.4 | async-start | bytes 2129920 | tf_op jit(solution)/shard_map/all_gather | solution.py:90
  144.4 338.8 %reduce-scatter.2.cloned.1.call-start = ((), (), s32[]{:S(2)}) async-start(), calls=%async_computation.5 | async-start | bytes 327680 | tf_op jit(solution)/shard_map/reduce_scatter | solution.py:94
Sparse Core Ops, SparseCore 0:
  144.5 261.1 all-gather.1
  408.9 74.3 reduce-scatter.1
where the time goes:
time: 492 us; the launch traced here: 490 us
  waiting for transfers between devices  355 us (72%)
  matrix products  53.1 us (11%)
  blocking collectives  23.6 us (5%)
  between operations  14.2 us (3%)
  local copies, waits for them, and re-layouts  12.7 us (3%)
  starting transfers between devices  11.5 us (2%)
  other arithmetic  10.7 us (2%)
  loops' own time  9.3 us (2%)
    all_gather x1, waiting for transfers between devices, per_device(): lax.all_gather(attended, ('ctx', 'sess'), axis=0, tiled=True)  261 us
    reduce_scatter x1, waiting for transfers between devices, per_device(): lax.psum_scatter(partial_out, 'head', scatter_dimension=0, tiled=True)  74.5 us
    dot_general x16, matrix products, online_update(): jnp.einsum(einsum_form, weights.astype(jnp.bfloat16), values, preferred_e...  26.5 us
    all_gather x1, blocking collectives, per_device(): gathered = lax.all_gather(queries, 'ctx', axis=0, tiled=True)  23.6 us
    dot_general x12, matrix products, prefix_step(): jnp.einsum('rkgd,knd->rkgn', grouped, key_block, preferred_element_type=j...  17.7 us
  transfers between devices with their start and end apart: 5, of which 5 were waited for; matrix products, arithmetic and copies ran while one was open for 1% of the time, Pallas kernels for 0%

commit v1 on v0

--- a/solution.py
+++ b/solution.py
@@ -25,7 +25,24 @@
     head_dim = queries.shape[2]
     group_size = queries.shape[1] // kv_local
     score_scale = 1.0 / math.sqrt(head_dim)
-    gathered = lax.all_gather(queries, "ctx", axis=0, tiled=True)
+    peers, position_2, rows = (lax.axis_size("ctx"), lax.axis_index("ctx"), queries.shape[0])
+    upward = [(i, (i + 1) % peers) for i in range(peers)]
+    left = [(i, (i - 1) % peers) for i in range(peers)]
+    filled = jnp.zeros((*queries.shape[:0], peers * rows, *queries.shape[0 + 1 :]), queries.dtype)
+    filled = lax.dynamic_update_slice_in_dim(filled, queries, position_2 * rows, axis=0)
+    from_left = from_right = queries
+    half = peers // 2
+    for step in range(1, half + 1):
+        from_left = lax.ppermute(from_left, "ctx", upward)
+        filled = lax.dynamic_update_slice_in_dim(
+            filled, from_left, (position_2 - step) % peers * rows, axis=0
+        )
+        if step < peers - half:
+            from_right = lax.ppermute(from_right, "ctx", left)
+            filled = lax.dynamic_update_slice_in_dim(
+                filled, from_right, (position_2 + step) % peers * rows, axis=0
+            )
+    gathered = filled
     rows_total = gathered.shape[0]
     grouped = gathered.reshape(rows_total, kv_local, group_size, head_dim)
     prefix_len = prefix_keys.shape[1]

time: 492 us -> 487 us (0.990)
  blocking collectives: 23.6 us -> 0 us
  starting transfers between devices: 11.5 us -> 24 us
  waiting for transfers between devices: 355 us -> 360 us
    all_gather x1 -> x0, blocking collectives: 23.6 us -> none  [per_device(): gathered = lax.all_gather(queries, 'ctx', axis=0, tiled=True)]
    ppermute x0 -> x7, starting transfers between devices: none -> 11.8 us  [the longest x3 9.29 us: per_device(): from_right = lax.ppermute(from_right, 'ctx', left)]
    ppermute x0 -> x7, waiting for transfers between devices: none -> 6.9 us  [the longest x4 6.89 us: per_device(): from_left = lax.ppermute(from_left, 'ctx', upward)]
  transfers between devices with their start and end apart: 5 -> 12, of which waited for: 5 -> 9; matrix products, arithmetic and copies ran while one was open for 1% -> 1% of each run, Pallas kernels for 0% -> 0%
where the time goes in v1:
time: 487 us; the launch traced here: 486 us
  waiting for transfers between devices  360 us (74%)
  matrix products  53.2 us (11%)
  starting transfers between devices  24 us (5%)
  between operations  14.5 us (3%)
  local copies, waits for them, and re-layouts  13.6 us (3%)
  other arithmetic  10.7 us (2%)
  loops' own time  9.3 us (2%)
    all_gather x1, waiting for transfers between devices, per_device(): lax.all_gather(attended, ('ctx', 'sess'), axis=0, tiled=True)  260 us
    reduce_scatter x1, waiting for transfers between devices, per_device(): lax.psum_scatter(partial_out, 'head', scatter_dimension=0, tiled=True)  74.5 us
    dot_general x16, matrix products, online_update(): jnp.einsum(einsum_form, weights.astype(jnp.bfloat16), values, preferred_e...  26.5 us
    dot_general x12, matrix products, prefix_step(): jnp.einsum('rkgd,knd->rkgn', grouped, key_block, preferred_element_type=j...  17.7 us
  transfers between devices with their start and end apart: 12, of which 9 were waited for; matrix products, arithmetic and copies ran while one was open for 1% of the time, Pallas kernels for 0%

profile of v1, /device:TPU:1, one launch (start us, length us, event | category | flops | bytes accessed | tf_op | source)
XLA Modules:
  0.0 485.6 jit_solution(17943010362695496835)
XLA Ops:
  6.5 2.5 collective-permute-start
  9.0 3.9 collective-permute-start.1
  14.5 2.7 collective-permute-start.3
  18.4 2.7 collective-permute-start.5
  22.5 3.9 collective-permute-done.6
  26.4 63.3 %while.30 = (s32[]{:T(128)}, f32[64,2,8]{0,2,1:T(8,128)S(1)}, f32[64,2,8]{0,2,1:T(8,128)S(1)}, f32[64,2,8,128]{3,0,2,1:T(8,128)S(1)}, s32[12]{0:T(128)S(1)}, /*i...) while((s32[]{:T(128)}, f32[64,2,8]{0,2,1:T(8,128)S(1)}, ...), condition=%wide.region_3.4_spmd.clone, body=%wide.region_0.3_spmd.clone.sunk | while | flops 273028096 | bytes 8192195 | solution.py:66
  35.2 1.8 fusion.55
  40.5 1.8 fusion.55
  45.7 1.8 fusion.55
  51.0 1.8 fusion.55
  56.3 1.8 fusion.55
  61.5 1.8 fusion.55
  66.8 1.8 fusion.55
  72.1 1.8 fusion.55
  90.6 5.3 %all-to-all-start = ((f32[8,1,128]{2,1,0:T(1,128)}), f32[8,1,128]{2,1,0:T(1,128)S(1)}, u32[]{:S(2)}, u32[]{:S(2)}) async-start(f32[8,1,128]{2,1,0:T(1,128)} %reshape.67), calls=%async_computation | async-start | bytes 8192 | tf_op jit(solution)/shard_map/all_to_all | solution.py:71
  96.7 5.6 %all-to-all-done = f32[8,1,128]{2,1,0:T(1,128)S(1)} async-done(((f32[8,1,128]{2,1,0:T(1,128)}), f32[8,1,128]{2,1,0:T(1,128)S(1)}, u32[]{:S(2)}, u32[]{:S(2)}) %all-to-all-start) | async-done | bytes 4128 | tf_op jit(solution)/shard_map/all_to_all | solution.py:71
  102.3 3.3 all-to-all-start.1
  106.7 5.3 %all-to-all-done.1 = f32[8,1,128]{2,1,0:T(1,128)S(1)} async-done(((f32[8,1,128]{2,1,0:T(1,128)}), f32[8,1,128]{2,1,0:T(1,128)S(1)}, u32[]{:S(2)}, u32[]{:S(2)}) %all-to-all-start.1) | async-done | bytes 4128 | tf_op jit(solution)/shard_map/all_to_all | solution.py:72
  112.1 3.5 all-to-all-start.2
  119.4 8.3 %all-to-all-done.2 = f32[64,2,8,128]{3,2,1,0:T(8,128)S(1)} async-done(((f32[64,2,8,128]{3,2,1,0:T(8,128)}), f32[64,2,8,128]{3,2,1,0:T(8,128)S(1)}, u32[]{:S(2)}, u32[]{:S(2)}) %all-to-all-start.2) | async-done | bytes 524320 | tf_op jit(solution)/shard_map/all_to_all | solution.py:73
  127.9 12.8 %while.29 = (s32[]{:T(128)}, f32[8,2,8]{2,1,0:T(2,128)S(1)}, f32[8,2,8]{2,1,0:T(2,128)S(1)}, f32[8,2,8,128]{3,2,1,0:T(8,128)S(1)}, s32[]{:T(128)}, /*index=5*/s3...) while((s32[]{:T(128)}, f32[8,2,8]{2,1,0:T(2,128)S(1)}, ...), condition=%wide.region_11.12_spmd, body=%wide.region_8.11_spmd.sunk | while | flops 8537478 | bytes 1420503 | solution.py:103
  141.4 259.8 %all-gather.2.cloned.1.call-done = bf16[512,2048]{1,0:T(8,128)(2,1)} async-done(((bf16[8,2048]{1,0:T(8,128)(2,1)}), bf16[512,2048]{1,0:T(8,128)(2,1)}) %all-gather.2.cloned.1.call-update) | async-done | bytes 2097168 | tf_op jit(solution)/shard_map/all_gather | solution.py:107
  401.2 3.0 fusion.29
  404.3 74.5 %reduce-scatter.2.cloned.1.call-done = f32[128,128]{1,0:T(8,128)} async-done(((f32[512,128]{1,0:T(8,128)}), f32[128,128]{1,0:T(8,128)}) %reduce-scatter.2.cloned.1.call-update) | async-done | bytes 65552 | tf_op jit(solution)/shard_map/reduce_scatter | solution.py:111
  (161 shorter events, 63.5 us)
Async XLA Ops:
  6.5 394.7 %copy-start = (bf16[2048,128]{1,0:T(8,128)(2,1)S(1)}, bf16[2048,128]{1,0:T(8,128)(2,1)}, u32[]{:S(2)}) copy-start(bf16[2048,128]{1,0:T(8,128)(2,1)} %param.17) | copy-start | bytes 1572868
  6.5 7.9 %collective-permute-start = (bf16[8,16,128]{2,1,0:T(8,128)(2,1)}, bf16[8,16,128]{2,1,0:T(8,128)(2,1)S(1)}, u32[]{:S(2)}, u32[]{:S(2)}) collective-permute-start(bf16[8,16,128]{2,1,0:T(8,128)(2,1)} %param.11), channel_id=1, source_target_pairs={{0,32},{32,64},{64,96},{96,128},{128,160},{160,192},{192,224},{224... | collective-permute-start | bytes 98312 | tf_op jit(solution)/shard_map/ppermute | solution.py:36
  9.0 5.5 %collective-permute-start.1 = (bf16[8,16,128]{2,1,0:T(8,128)(2,1)}, bf16[8,16,128]{2,1,0:T(8,128)(2,1)S(1)}, u32[]{:S(2)}, u32[]{:S(2)}) collective-permute-start(bf16[8,16,128]{2,1,0:T(8,128)(2,1)} %param.11), channel_id=1, source_target_pairs={{0,224},{32,0},{64,32},{96,64},{128,96},{160,128},{192,160},{224,1... | collective-permute-start | bytes 98312 | tf_op jit(solution)/shard_map/ppermute | solution.py:41
  14.5 4.0 collective-permute-start.2
  14.5 4.0 collective-permute-start.3
  18.4 4.0 collective-permute-start.4
  18.4 4.0 collective-permute-start.5
  22.4 4.0 collective-permute-start.6
  89.7 25.9 %copy-start.2 = (s32[8]{0:T(128)S(1)}, s32[8]{0:T(128)}, u32[]{:S(2)}) copy-start(s32[8]{0:T(128)} %param.16) | copy-start | bytes 100
  89.7 38.2 %copy-start.1 = (bf16[8,16,128]{2,1,0:T(8,128)(2,1)S(1)}, bf16[8,16,128]{2,1,0:T(8,128)(2,1)}, u32[]{:S(2)}) copy-start(bf16[8,16,128]{2,1,0:T(8,128)(2,1)} %param.11) | copy-start | bytes 98308
  90.6 11.7 %all-to-all-start = ((f32[8,1,128]{2,1,0:T(1,128)}), f32[8,1,128]{2,1,0:T(1,128)S(1)}, u32[]{:S(2)}, u32[]{:S(2)}) async-start(f32[8,1,128]{2,1,0:T(1,128)} %reshape.67), calls=%async_computation | async-start | bytes 8192 | tf_op jit(solution)/shard_map/all_to_all | solution.py:71
  102.3 9.8 %all-to-all-start.1 = ((f32[8,1,128]{2,1,0:T(1,128)}), f32[8,1,128]{2,1,0:T(1,128)S(1)}, u32[]{:S(2)}, u32[]{:S(2)}) async-start(f32[8,1,128]{2,1,0:T(1,128)} %reshape.69), calls=%async_computation.1 | async-start | bytes 8192 | tf_op jit(solution)/shard_map/all_to_all | solution.py:72
  112.1 15.6 %all-to-all-start.2 = ((f32[64,2,8,128]{3,2,1,0:T(8,128)}), f32[64,2,8,128]{3,2,1,0:T(8,128)S(1)}, u32[]{:S(2)}, u32[]{:S(2)}) async-start(f32[64,2,8,128]{3,2,1,0:T(8,128)} %copy.30), calls=%async_computation.2 | async-start | bytes 1048576 | tf_op jit(solution)/shard_map/all_to_all | solution.py:73
  115.6 285.7 %all-gather.2.cloned.1.call-start = ((), (), s32[]{:S(2)}) async-start(), calls=%async_computation.4 | async-start | bytes 2129920 | tf_op jit(solution)/shard_map/all_gather | solution.py:107
  141.4 337.4 %reduce-scatter.2.cloned.1.call-start = ((), (), s32[]{:S(2)}) async-start(), calls=%async_computation.5 | async-start | bytes 327680 | tf_op jit(solution)/shard_map/reduce_scatter | solution.py:111
Sparse Core Ops, SparseCore 0:
  141.5 259.6 all-gather.1
  404.4 74.3 reduce-scatter.1
